TPU v7x, 256 devices: a whole 4x4x8 slice. The times are simulated.
256 devices in a mesh: wide: 32 (over x, y, core), narrow: 8 (over z).
Axes of the slice: x: 4, y: 4, z: 8, core: 2. Of those that a mesh axis runs over, the one named last changes fastest.
Arguments:
- panels: float32 [256, 512, 512], P('wide', 'narrow'), may hold values from -0.6 to 0.6
- factors: float32 [64, 512, 512], P('wide', 'narrow'), may hold values from -2 to 2
- member: int32 [64, 4], replicated, may hold values from 0 to 255, as said below
- target: int32 [64, 10], replicated, may hold values from 0 to 31
- ancestors: float32 [32, 512, 512], P('wide', 'narrow'), may hold values from -6 to 6
Outputs:
- updated: float32 [32, 512, 512], P('wide', 'narrow')
Inputs may be any that keep to these rules, and one draw needn't show every extreme that they name: `member`: the blocks of supernode s are 4 distinct indices in [(s // 2) * 8, (s // 2 + 1) * 8); every block belongs to exactly one supernode.
All inputs are finite; a program needn't handle non-finite values.
Results may differ from a plain program's by a relative error of at most 0.0003.
Values sent between devices are 32-bit elements; how exact they have to be, the bound alone decides.
No kernel may reach another device: no remote copies, remote signals or barrier semaphores. Data moves between devices by JAX's collectives and lax.ppermute only.
A program may use at most 128 MiB of HBM per device.

v0:
```python
import jax
import jax.numpy as jnp
import numpy as np
from jax import lax
from jax.sharding import PartitionSpec as P


def pair_lists(count):
    left_pick = []
    right_pick = []
    for upper in range(count):
        for lower in range(upper + 1):
            left_pick.append(upper)
            right_pick.append(lower)
    return (np.array(left_pick, dtype=np.int32), np.array(right_pick, dtype=np.int32))


def shards(panels, factors, member, target, ancestors):
    highest = lax.Precision.HIGHEST
    sup_count = factors.shape[0]
    blk_count = panels.shape[0]
    tile_count = ancestors.shape[0] * lax.axis_size("wide")
    left_pick, right_pick = pair_lists(member.shape[1])
    owner_index = lax.axis_index("wide")
    own_members = (
        lax.dynamic_slice_in_dim(member, owner_index * sup_count, sup_count, 0)
        - owner_index * blk_count
    )
    own_targets = lax.dynamic_slice_in_dim(target, owner_index * sup_count, sup_count, 0)
    full_factors = lax.all_gather(factors, "narrow", axis=1, tiled=True)
    blocks = panels[own_members]
    scaled = jnp.einsum("skrw,swv->skrv", blocks, full_factors, precision=highest)
    left_rows = scaled[:, left_pick]
    right_rows = lax.all_gather(scaled, "narrow", axis=2, tiled=True)[:, right_pick]
    updates = jnp.einsum("sprv,spmv->sprm", left_rows, right_rows, precision=highest)
    tile_ids = jnp.arange(tile_count, dtype=jnp.int32)
    onehot = (own_targets[:, :, None] == tile_ids[None, None, :]).astype(jnp.float32)
    portion = jnp.einsum("spa,sprw->arw", onehot, updates, precision=highest)
    totals = lax.psum_scatter(portion, "wide", scatter_dimension=0, tiled=True)
    return ancestors - totals


def solution(mesh):
    return jax.shard_map(
        shards,
        mesh=mesh,
        in_specs=(
            P("wide", "narrow", None),
            P("wide", "narrow", None),
            P(),
            P(),
            P("wide", "narrow", None),
        ),
        out_specs=P("wide", "narrow", None),
        check_vma=False,
    )
```

profile of v0, /device:TPU:2, one launch (start us, length us, event | category | flops | bytes accessed | tf_op | source)
XLA Modules:
  0.0 293.5 jit_solution(6393277430765025806)
XLA Ops:
  6.5 0.7 all-gather.3.cloned.1.call-update
  7.3 0.0 all-gather.5.cloned.1.call-start
  7.3 0.8 compare_select_fusion
  8.1 0.1 copy.15
  8.2 0.1 reshape.3
  8.3 0.0 copy-done
  8.3 0.6 gather_fusion
  8.9 44.1 %all-gather.3.cloned.1.call-done = f32[2,512,512]{2,1,0:T(8,128)} async-done(((f32[2,64,512]{2,1,0:T(8,128)}), f32[2,512,512]{2,1,0:T(8,128)}) %all-gather.3.cloned.1.call-update) | async-done | bytes 2097168 | tf_op jit(solution)/shard_map/all_gather | solution.py:30
  53.0 4.5 %fusion.8 = f32[2,4,64,512]{3,2,1,0:T(8,128)} fusion(f32[2,4,64,512]{3,2,1,0:T(8,128)S(1)} %bitcast.21, f32[2,512,512]{2,1,0:T(8,128)} %all-gather.3.cloned.1.call-done), kind=kOutput, calls=%fused_computation.9 | convolution fusion | flops 1610612736 | bytes 4194304 | tf_op jit(solution)/shard_map/skrw,swv->skrv/dot_general | solution.py:32
  57.5 0.0 all-gather.5.cloned.1.call-update
  57.6 0.0 reduce-scatter.2.cloned.1.call-start
  57.6 0.0 copy-done.3
  57.6 0.1 constant_dynamic-slice_fusion
  57.7 0.1 copy.14
  57.8 0.9 copy-done.1
  58.8 2.2 gather_fusion.1
  60.9 89.4 %all-gather.5.cloned.1.call-done = f32[2,4,512,512]{3,2,1,0:T(8,128)} async-done(((f32[2,4,64,512]{3,2,1,0:T(8,128)}), f32[2,4,512,512]{3,2,1,0:T(8,128)}) %all-gather.5.cloned.1.call-update) | async-done | bytes 8388624 | tf_op jit(solution)/shard_map/all_gather | solution.py:34
  150.3 12.6 %gather_fusion.2 = f32[10,2,512,512]{3,2,1,0:T(8,128)} fusion(f32[2,4,512,512]{3,2,1,0:T(8,128)} %all-gather.5.cloned.1.call-done, s32[1024]{0:T(1024)S(1)} %pad_clamp_fusion), kind=kCustom, calls=%fused_computation.2 | custom fusion | bytes 41943080 | tf_op jit(solution)/shard_map/gather | solution.py:34
  162.9 25.8 %fusion = f32[2,10,64,512]{3,2,1,0:T(8,128)S(1)} fusion(f32[10,2,512,512]{3,2,1,0:T(8,128)} %gather_fusion.2, f32[10,2,64,512]{3,2,1,0:T(8,128)} %gather_fusion.1), kind=kOutput, calls=%fused_computation.3 | convolution fusion | flops 4026531840 | bytes 26214400 | tf_op jit(solution)/shard_map/sprv,spmv->sprm/dot_general | solution.py:35
  188.7 3.9 %fusion.5 = f32[32,64,512]{2,0,1:T(8,128)S(1)} fusion(f32[2,10,64,512]{3,2,1,0:T(8,128)S(1)} %fusion, s32[2,10]{1,0:T(2,128)S(1)} %copy.14), kind=kOutput, calls=%fused_computation.8 | convolution fusion | flops 251658880 | bytes 6815824 | tf_op jit(solution)/shard_map/spa,sprw->arw/dot_general | solution.py:38
  192.6 4.4 %copy.16 = f32[32,64,512]{2,1,0:T(8,128)} copy(f32[32,64,512]{2,0,1:T(8,128)S(1)} %fusion.5) | data formatting | bytes 8388608 | tf_op jit(solution)/shard_map/spa,sprw->arw/dot_general | solution.py:38
  197.0 0.0 reduce-scatter.2.cloned.1.call-update
  197.0 88.4 %reduce-scatter.2.cloned.1.call-done = f32[1,64,512]{2,1,0:T(8,128)} async-done(((f32[32,64,512]{2,1,0:T(8,128)}), f32[1,64,512]{2,1,0:T(8,128)}) %reduce-scatter.2.cloned.1.call-update) | async-done | bytes 131088 | tf_op jit(solution)/shard_map/reduce_scatter | solution.py:39
  285.4 1.6 sub.11
  (13 shorter events, 0.0 us)
Async XLA Ops:
  6.5 1.7 copy-start
  6.5 46.4 %all-gather.3.cloned.1.call-start = ((), (), s32[]{:S(2)}) async-start(), calls=%async_computation.1 | async-start | bytes 2359296 | tf_op jit(solution)/shard_map/all_gather | solution.py:30
  7.3 143.1 %all-gather.5.cloned.1.call-start = ((), (), s32[]{:S(2)}) async-start(), calls=%async_computation.2 | async-start | bytes 9437184 | tf_op jit(solution)/shard_map/all_gather | solution.py:34
  53.0 4.6 %copy-start.3 = (s32[64,10]{0,1:T(8,128)S(1)}, s32[64,10]{0,1:T(8,128)}, u32[]{:S(2)}) copy-start(s32[64,10]{0,1:T(8,128)} %param.12) | copy-start | bytes 7684
  53.0 4.8 %copy-start.5 = (s32[10]{0:T(128)S(1)}, s32[10]{0:T(128)}, u32[]{:S(2)}) copy-start(s32[10]{0:T(128)} %constant.33) | copy-start | bytes 124
  53.0 4.8 %copy-start.4 = (s32[10]{0:T(128)S(1)}, s32[10]{0:T(128)}, u32[]{:S(2)}) copy-start(s32[10]{0:T(128)} %constant.32) | copy-start | bytes 124
  57.5 1.2 copy-start.1
  57.6 227.9 %reduce-scatter.2.cloned.1.call-start = ((), (), s32[]{:S(2)}) async-start(), calls=%async_computation.3 | async-start | bytes 4325376 | tf_op jit(solution)/shard_map/reduce_scatter | solution.py:39
  197.0 88.4 %copy-start.2 = (f32[1,64,512]{2,1,0:T(8,128)S(1)}, f32[1,64,512]{2,1,0:T(8,128)}, u32[]{:S(2)}) copy-start(f32[1,64,512]{2,1,0:T(8,128)} %param.13) | copy-start | bytes 393220
Sparse Core Ops, SparseCore 0:
  9.1 43.8 all-gather.2
  57.7 92.6 all-gather.4
  197.1 88.2 reduce-scatter.1
where the time goes:
time: 294 us
  waiting for transfers between devices  223 us (76%)
  matrix products  34.2 us (12%)
  local copies, waits for them, and re-layouts  21.1 us (7%)
  between operations  13.2 us (4%)
    all_gather x1, waiting for transfers between devices, shards(): lax.all_gather(scaled, 'narrow', axis=2, tiled=True)[:, right_pick]  89.4 us
    reduce_scatter x1, waiting for transfers between devices, shards(): totals = lax.psum_scatter(portion, 'wide', scatter_dimension=0, tiled=True)  88.4 us
    all_gather x1, waiting for transfers between devices, shards(): full_factors = lax.all_gather(factors, 'narrow', axis=1, tiled=True)  44.1 us
    dot_general x1, matrix products, shards(): jnp.einsum('sprv,spmv->sprm', left_rows, right_rows, precision=highest)  25.8 us
    gather x1, local copies, waits for them, and re-layouts, shards(): lax.all_gather(scaled, 'narrow', axis=2, tiled=True)[:, right_pick]  12.6 us
  transfers between devices with their start and end apart: 3, of which 3 were waited for; matrix products, arithmetic and copies ran while one was open for 1% of the time, Pallas kernels for 0%

commit v1 on v0

--- a/solution.py
+++ b/solution.py
@@ -3,6 +3,22 @@
 import numpy as np
 from jax import lax
 from jax.sharding import PartitionSpec as P
+
+
+def ring_product(value, axis, dim, contribution):
+    length, place, width = (lax.axis_size(axis), lax.axis_index(axis), value.shape[dim])
+    upward = [(i, (i + 1) % length) for i in range(length)]
+    left = [(i, (i - 1) % length) for i in range(length)]
+    half = length // 2
+    from_left = from_right = value
+    running = contribution(value, place * width)
+    for step in range(1, half + 1):
+        from_left = lax.ppermute(from_left, axis, upward)
+        if step < length - half:
+            from_right = lax.ppermute(from_right, axis, left)
+            running = running + contribution(from_right, (place + step) % length * width)
+        running = running + contribution(from_left, (place - step) % length * width)
+    return running
 
 
 def pair_lists(count):
@@ -27,9 +43,18 @@
         - owner_index * blk_count
     )
     own_targets = lax.dynamic_slice_in_dim(target, owner_index * sup_count, sup_count, 0)
-    full_factors = lax.all_gather(factors, "narrow", axis=1, tiled=True)
     blocks = panels[own_members]
-    scaled = jnp.einsum("skrw,swv->skrv", blocks, full_factors, precision=highest)
+    scaled = ring_product(
+        factors,
+        "narrow",
+        1,
+        lambda shard, at: jnp.einsum(
+            "skrw,swv->skrv",
+            lax.dynamic_slice_in_dim(blocks, at, shard.shape[1], axis=3),
+            shard,
+            precision=highest,
+        ),
+    )
     left_rows = scaled[:, left_pick]
     right_rows = lax.all_gather(scaled, "narrow", axis=2, tiled=True)[:, right_pick]
     updates = jnp.einsum("sprv,spmv->sprm", left_rows, right_rows, precision=highest)

time: 294 us -> 282 us (0.959)
  waiting for transfers between devices: 223 us -> 192 us
  starting transfers between devices: 0.08 us -> 12.5 us
  matrix products: 34.2 us -> 39.9 us
    all_gather x1 -> x0, waiting for transfers between devices: 44.1 us -> none  [shards(): full_factors = lax.all_gather(factors, 'narrow', axis=1, tiled=True)]
    ppermute x0 -> x7, waiting for transfers between devices: none -> 15.9 us  [the longest x4 15.9 us: ring_product(): from_left = lax.ppermute(from_left, axis, upward)]
    ppermute x0 -> x7, starting transfers between devices: none -> 12.4 us  [the longest x3 12.4 us: ring_product(): from_right = lax.ppermute(from_right, axis, left)]
    dot_general x1 -> x8, matrix products: 4.54 us -> 10.2 us  [shards(): jnp.einsum('skrw,swv->skrv', lax.dynamic_slice_in_dim(blocks, at, shard.s...]
  transfers between devices with their start and end apart: 3 -> 9, of which waited for: 3 -> 6; matrix products, arithmetic and copies ran while one was open for 1% -> 5% of each run, Pallas kernels for 0% -> 0%
where the time goes in v1:
time: 282 us
  waiting for transfers between devices  192 us (68%)
  matrix products  39.9 us (14%)
  local copies, waits for them, and re-layouts  21.4 us (8%)
  between operations  13.6 us (5%)
  starting transfers between devices  12.5 us (4%)
    reduce_scatter x1, waiting for transfers between devices, shards(): totals = lax.psum_scatter(portion, 'wide', scatter_dimension=0, tiled=True)  88.4 us
    all_gather x1, waiting for transfers between devices, shards(): lax.all_gather(scaled, 'narrow', axis=2, tiled=True)[:, right_pick]  88.1 us
    dot_general x1, matrix products, shards(): jnp.einsum('sprv,spmv->sprm', left_rows, right_rows, precision=highest)  25.8 us
    ppermute x4, waiting for transfers between devices, ring_product(): from_left = lax.ppermute(from_left, axis, upward)  15.9 us
    gather x1, local copies, waits for them, and re-layouts, shards(): lax.all_gather(scaled, 'narrow', axis=2, tiled=True)[:, right_pick]  12.6 us
    ppermute x3, starting transfers between devices, ring_product(): from_right = lax.ppermute(from_right, axis, left)  12.4 us
    dot_general x8, matrix products, shards(): jnp.einsum('skrw,swv->skrv', lax.dynamic_slice_in_dim(blocks, at, shard.s...  10.2 us
  transfers between devices with their start and end apart: 9, of which 6 were waited for; matrix products, arithmetic and copies ran while one was open for 5% of the time, Pallas kernels for 0%

profile of v1, /device:TPU:2, one launch (start us, length us, event | category | flops | bytes accessed | tf_op | source)
XLA Modules:
  0.0 282.2 jit_solution(4167703075052496583)
XLA Ops:
  6.5 5.9 %collective-permute-start = (f32[2,64,512]{2,1,0:T(8,128)}, f32[2,64,512]{2,1,0:T(8,128)S(1)}, u32[]{:S(2)}, u32[]{:S(2)}) collective-permute-start(f32[2,64,512]{2,1,0:T(8,128)} %param.10), channel_id=1, source_target_pairs={{0,7},{1,0},{2,1},{3,2},{4,3},{5,4},{6,5},{7,6},{8,15},{9,8},{10,9... | collective-permute-start | bytes 786440 | tf_op jit(solution)/shard_map/ppermute | solution.py:18
  12.4 0.8 compare_select_fusion
  14.1 2.0 fusion.19
  16.0 5.5 %collective-permute-done.1 = f32[2,64,512]{2,1,0:T(8,128)S(1)} collective-permute-done((f32[2,64,512]{2,1,0:T(8,128)}, f32[2,64,512]{2,1,0:T(8,128)S(1)}, u32[]{:S(2)}, u32[]{:S(2)}) %collective-permute-start.1) | collective-permute-done | bytes 262176 | tf_op jit(solution)/shard_map/ppermute | solution.py:16
  21.6 3.2 %collective-permute-start.2 = (f32[2,64,512]{2,1,0:T(8,128)S(1)}, f32[2,64,512]{2,1,0:T(8,128)S(1)}, u32[]{:S(2)}, u32[]{:S(2)}) collective-permute-start(f32[2,64,512]{2,1,0:T(8,128)S(1)} %collective-permute-done), channel_id=1, source_target_pairs={{0,7},{1,0},{2,1},{3,2},{4,3},{5,4},{6,5},{7,6},{8,15},{9,8},{10,9... | collective-permute-start | bytes 786440 | tf_op jit(solution)/shard_map/ppermute | solution.py:18
  24.8 1.0 convolution_add_fusion.4
  25.9 1.0 convolution_add_fusion.3
  26.9 2.8 collective-permute-done.3
  29.7 1.0 fusion.14
  30.8 3.3 %collective-permute-start.4 = (f32[2,64,512]{2,1,0:T(8,128)S(1)}, f32[2,64,512]{2,1,0:T(8,128)S(1)}, u32[]{:S(2)}, u32[]{:S(2)}) collective-permute-start(f32[2,64,512]{2,1,0:T(8,128)S(1)} %collective-permute-done.2), channel_id=1, source_target_pairs={{0,7},{1,0},{2,1},{3,2},{4,3},{5,4},{6,5},{7,6},{8,15},{9,8},{10,9... | collective-permute-start | bytes 786440 | tf_op jit(solution)/shard_map/ppermute | solution.py:18
  34.1 1.1 fusion.9
  35.2 2.1 collective-permute-done.5
  37.3 1.0 fusion.11
  38.3 1.1 fusion.8
  39.4 5.5 %collective-permute-done.6 = f32[2,64,512]{2,1,0:T(8,128)S(1)} collective-permute-done((f32[2,64,512]{2,1,0:T(8,128)S(1)}, f32[2,64,512]{2,1,0:T(8,128)S(1)}, u32[]{:S(2)}, u32[]{:S(2)}) %collective-permute-start.6) | collective-permute-done | bytes 262176 | tf_op jit(solution)/shard_map/ppermute | solution.py:16
  44.9 2.0 convolution_add_fusion
  47.2 3.4 %gather_fusion.1 = f32[10,2,64,512]{3,2,1,0:T(8,128)} fusion(f32[2,4,64,512]{3,2,1,0:T(8,128)} %convolution_add_fusion, s32[1024]{0:T(1024)S(1)} %pad_clamp_fusion.1), kind=kCustom, calls=%fused_computation.1 | custom fusion | bytes 5242920 | tf_op jit(solution)/shard_map/gather | solution.py:58
  50.6 88.1 %all-gather.2.cloned.1.call-done = f32[2,4,512,512]{3,2,1,0:T(8,128)} async-done(((f32[2,4,64,512]{3,2,1,0:T(8,128)}), f32[2,4,512,512]{3,2,1,0:T(8,128)}) %all-gather.2.cloned.1.call-update) | async-done | bytes 8388624 | tf_op jit(solution)/shard_map/all_gather | solution.py:59
  138.7 12.6 %gather_fusion.2 = f32[10,2,512,512]{3,2,1,0:T(8,128)} fusion(f32[2,4,512,512]{3,2,1,0:T(8,128)} %all-gather.2.cloned.1.call-done, s32[1024]{0:T(1024)S(1)} %pad_clamp_fusion), kind=kCustom, calls=%fused_computation.2 | custom fusion | bytes 41943080 | tf_op jit(solution)/shard_map/gather | solution.py:59
  151.3 25.8 %fusion = f32[2,10,64,512]{3,2,1,0:T(8,128)S(1)} fusion(f32[10,2,512,512]{3,2,1,0:T(8,128)} %gather_fusion.2, f32[10,2,64,512]{3,2,1,0:T(8,128)} %gather_fusion.1), kind=kOutput, calls=%fused_computation.3 | convolution fusion | flops 4026531840 | bytes 26214400 | tf_op jit(solution)/shard_map/sprv,spmv->sprm/dot_general | solution.py:60
  177.1 3.9 %fusion.5 = f32[32,64,512]{2,0,1:T(8,128)S(1)} fusion(f32[2,10,64,512]{3,2,1,0:T(8,128)S(1)} %fusion, s32[2,10]{1,0:T(2,128)S(1)} %copy.14), kind=kOutput, calls=%fused_computation.8 | convolution fusion | flops 251658880 | bytes 6815824 | tf_op jit(solution)/shard_map/spa,sprw->arw/dot_general | solution.py:63
  181.0 4.4 %copy.16 = f32[32,64,512]{2,1,0:T(8,128)} copy(f32[32,64,512]{2,0,1:T(8,128)S(1)} %fusion.5) | data formatting | bytes 8388608 | tf_op jit(solution)/shard_map/spa,sprw->arw/dot_general | solution.py:63
  185.4 88.4 %reduce-scatter.2.cloned.1.call-done = f32[1,64,512]{2,1,0:T(8,128)} async-done(((f32[32,64,512]{2,1,0:T(8,128)}), f32[1,64,512]{2,1,0:T(8,128)}) %reduce-scatter.2.cloned.1.call-update) | async-done | bytes 131088 | tf_op jit(solution)/shard_map/reduce_scatter | solution.py:64
  273.8 1.6 sub.27
  (29 shorter events, 1.1 us)
Async XLA Ops:
  6.5 6.9 %copy-start = (f32[8,64,512]{2,1,0:T(8,128)S(1)}, f32[8,64,512]{2,1,0:T(8,128)}, u32[]{:S(2)}) copy-start(f32[8,64,512]{2,1,0:T(8,128)} %param.9) | copy-start | bytes 3145732
  6.5 132.1 %all-gather.2.cloned.1.call-start = ((), (), s32[]{:S(2)}) async-start(), calls=%async_computation.1 | async-start | bytes 9437184 | tf_op jit(solution)/shard_map/all_gather | solution.py:59
  6.5 15.1 %collective-permute-start = (f32[2,64,512]{2,1,0:T(8,128)}, f32[2,64,512]{2,1,0:T(8,128)S(1)}, u32[]{:S(2)}, u32[]{:S(2)}) collective-permute-start(f32[2,64,512]{2,1,0:T(8,128)} %param.10), channel_id=1, source_target_pairs={{0,7},{1,0},{2,1},{3,2},{4,3},{5,4},{6,5},{7,6},{8,15},{9,8},{10,9... | collective-permute-start | bytes 786440 | tf_op jit(solution)/shard_map/ppermute | solution.py:18
  12.4 9.2 %collective-permute-start.1 = (f32[2,64,512]{2,1,0:T(8,128)}, f32[2,64,512]{2,1,0:T(8,128)S(1)}, u32[]{:S(2)}, u32[]{:S(2)}) collective-permute-start(f32[2,64,512]{2,1,0:T(8,128)} %param.10), channel_id=1, source_target_pairs={{0,1},{1,2},{2,3},{3,4},{4,5},{5,6},{6,7},{7,0},{8,9},{9,10},{10,1... | collective-permute-start | bytes 786440 | tf_op jit(solution)/shard_map/ppermute | solution.py:16
  21.6 8.1 %collective-permute-start.3 = (f32[2,64,512]{2,1,0:T(8,128)S(1)}, f32[2,64,512]{2,1,0:T(8,128)S(1)}, u32[]{:S(2)}, u32[]{:S(2)}) collective-permute-start(f32[2,64,512]{2,1,0:T(8,128)S(1)} %collective-permute-done.1), channel_id=1, source_target_pairs={{0,1},{1,2},{2,3},{3,4},{4,5},{5,6},{6,7},{7,0},{8,9},{9,10},{10,1... | collective-permute-start | bytes 786440 | tf_op jit(solution)/shard_map/ppermute | solution.py:16
  21.6 9.2 %collective-permute-start.2 = (f32[2,64,512]{2,1,0:T(8,128)S(1)}, f32[2,64,512]{2,1,0:T(8,128)S(1)}, u32[]{:S(2)}, u32[]{:S(2)}) collective-permute-start(f32[2,64,512]{2,1,0:T(8,128)S(1)} %collective-permute-done), channel_id=1, source_target_pairs={{0,7},{1,0},{2,1},{3,2},{4,3},{5,4},{6,5},{7,6},{8,15},{9,8},{10,9... | collective-permute-start | bytes 786440 | tf_op jit(solution)/shard_map/ppermute | solution.py:18
  29.7 7.6 %collective-permute-start.5 = (f32[2,64,512]{2,1,0:T(8,128)S(1)}, f32[2,64,512]{2,1,0:T(8,128)S(1)}, u32[]{:S(2)}, u32[]{:S(2)}) collective-permute-start(f32[2,64,512]{2,1,0:T(8,128)S(1)} %collective-permute-done.3), channel_id=1, source_target_pairs={{0,1},{1,2},{2,3},{3,4},{4,5},{5,6},{6,7},{7,0},{8,9},{9,10},{10,1... | collective-permute-start | bytes 786440 | tf_op jit(solution)/shard_map/ppermute | solution.py:16
  30.8 7.6 %collective-permute-start.4 = (f32[2,64,512]{2,1,0:T(8,128)S(1)}, f32[2,64,512]{2,1,0:T(8,128)S(1)}, u32[]{:S(2)}, u32[]{:S(2)}) collective-permute-start(f32[2,64,512]{2,1,0:T(8,128)S(1)} %collective-permute-done.2), channel_id=1, source_target_pairs={{0,7},{1,0},{2,1},{3,2},{4,3},{5,4},{6,5},{7,6},{8,15},{9,8},{10,9... | collective-permute-start | bytes 786440 | tf_op jit(solution)/shard_map/ppermute | solution.py:18
  35.1 11.8 %copy-start.2 = (s32[64,10]{0,1:T(8,128)S(1)}, s32[64,10]{0,1:T(8,128)}, u32[]{:S(2)}) copy-start(s32[64,10]{0,1:T(8,128)} %param.12) | copy-start | bytes 7684
  35.1 12.0 %copy-start.4 = (s32[10]{0:T(128)S(1)}, s32[10]{0:T(128)}, u32[]{:S(2)}) copy-start(s32[10]{0:T(128)} %constant.85) | copy-start | bytes 124
  35.2 12.0 %copy-start.3 = (s32[10]{0:T(128)S(1)}, s32[10]{0:T(128)}, u32[]{:S(2)}) copy-start(s32[10]{0:T(128)} %constant.84) | copy-start | bytes 124
  37.3 7.6 %collective-permute-start.6 = (f32[2,64,512]{2,1,0:T(8,128)S(1)}, f32[2,64,512]{2,1,0:T(8,128)S(1)}, u32[]{:S(2)}, u32[]{:S(2)}) collective-permute-start(f32[2,64,512]{2,1,0:T(8,128)S(1)} %collective-permute-done.5), channel_id=1, source_target_pairs={{0,1},{1,2},{2,3},{3,4},{4,5},{5,6},{6,7},{7,0},{8,9},{9,10},{10,1... | collective-permute-start | bytes 786440 | tf_op jit(solution)/shard_map/ppermute | solution.py:16
  46.9 226.9 %reduce-scatter.2.cloned.1.call-start = ((), (), s32[]{:S(2)}) async-start(), calls=%async_computation.2 | async-start | bytes 4325376 | tf_op jit(solution)/shard_map/reduce_scatter | solution.py:64
  185.4 88.4 %copy-start.1 = (f32[1,64,512]{2,1,0:T(8,128)S(1)}, f32[1,64,512]{2,1,0:T(8,128)}, u32[]{:S(2)}) copy-start(f32[1,64,512]{2,1,0:T(8,128)} %param.13) | copy-start | bytes 393220
Sparse Core Ops, SparseCore 0:
  47.0 91.6 all-gather.1
  185.5 88.2 reduce-scatter.1
